TPU v7x, 32 devices: a whole 2x2x4 slice. The times are simulated.
32 devices in a mesh: section: 4 (over z), tensor: 8 (over y, x, core).
Axes of the slice: x: 2, y: 2, z: 4, core: 2. Of those that a mesh axis runs over, the one named last changes fastest.
Arguments:
- resid: bfloat16 [32, 3584], P('tensor'), may hold values from -6 to 6
- w_enc: bfloat16 [7168, 3584], P(('section', 'tensor')), may hold values from -0.09375 to 0.09375
- b_enc: float32 [7168], P(('section', 'tensor')), may hold values from -1 to 0.5
- w_dec: bfloat16 [7168, 3584], P(('section', 'tensor')), may hold values from -0.0625 to 0.0625
- b_dec: float32 [3584], replicated, may hold values from -3 to 3
Outputs:
- recon: float32 [32, 3584], P('tensor')
- grad_w_dec: bfloat16 [7168, 3584], P(('section', 'tensor'))
- code_grad: float32 [32, 7168], P(None, ('section', 'tensor'))
- grad_b_dec: float32 [3584], replicated
- loss_value: float32 [], replicated
All inputs are finite; a program needn't handle non-finite values.
Results may differ from a plain program's by a relative error of at most 0.0032.
The roundings to bfloat16 on the way count: a program that leaves them out, or rounds other values in their place, can miss the bound.
Values may be sent and summed in bfloat16 or wider, within the bound.
No kernel may reach another device: no remote copies, remote signals or barrier semaphores. Data moves between devices by JAX's collectives and lax.ppermute only.
A program may use at most 64 MiB of HBM per device.

v0:
```python
import jax
import jax.numpy as jnp
from jax import lax
from jax.sharding import PartitionSpec as P

epsilon = 1e-06


def per_device(resid, w_enc, b_enc, w_dec, b_dec):
    stream = lax.all_gather(resid, "tensor", axis=0, tiled=True)
    preact = (
        lax.dot_general(stream, w_enc, (((1,), (1,)), ((), ())), preferred_element_type=jnp.float32)
        + b_enc
    )
    codes = jnp.maximum(preact, 0.0).astype(jnp.bfloat16)
    codes_f32 = codes.astype(jnp.float32)
    dec_f32 = w_dec.astype(jnp.float32)
    dec_norm = jnp.sqrt(jnp.sum(dec_f32 * dec_f32, axis=1) + epsilon)
    penalty = lax.psum(jnp.sum(codes_f32 * dec_norm), ("section", "tensor"))
    total_rows = stream.shape[0]
    model_width = stream.shape[1]
    shares = lax.psum_scatter(
        jnp.dot(codes, w_dec, preferred_element_type=jnp.float32),
        "tensor",
        scatter_dimension=0,
        tiled=True,
    )
    shares = lax.psum(shares, "section")
    recon = shares + b_dec
    errors = recon - resid.astype(jnp.float32)
    squares, grad_b_dec = lax.psum((jnp.sum(errors * errors), jnp.sum(errors, axis=0)), "tensor")
    err_half = lax.all_gather(errors.astype(jnp.bfloat16), "tensor", axis=0, tiled=True)
    loss_value = (0.5 * squares + penalty) / (total_rows * model_width)
    code_sums = jnp.sum(codes_f32, axis=0)
    grad_w_dec = lax.dot_general(
        codes, err_half, (((0,), (0,)), ((), ())), preferred_element_type=jnp.float32
    )
    grad_w_dec = grad_w_dec + code_sums[:, None] * dec_f32 / dec_norm[:, None]
    code_grad = (
        lax.dot_general(
            err_half, w_dec, (((1,), (1,)), ((), ())), preferred_element_type=jnp.float32
        )
        + dec_norm
    )
    return (recon, grad_w_dec.astype(jnp.bfloat16), code_grad, grad_b_dec, loss_value)


def solution(mesh):
    in_specs = (
        P("tensor", None),
        P(("section", "tensor"), None),
        P(("section", "tensor")),
        P(("section", "tensor"), None),
        P(),
    )
    out_specs = (
        P("tensor", None),
        P(("section", "tensor"), None),
        P(None, ("section", "tensor")),
        P(),
        P(),
    )
    return jax.shard_map(
        per_device, mesh=mesh, in_specs=in_specs, out_specs=out_specs, check_vma=False
    )
```

profile of v0, /device:TPU:0, one launch (start us, length us, event | category | flops | bytes accessed | tf_op | source)
XLA Modules:
  0.0 148.7 jit_solution(17115211651597049739)
XLA Ops:
  7.2 0.0 copy-start
  7.2 0.0 copy-start.2
  7.2 0.0 copy-start.6
  7.2 0.0 all-reduce.4.cloned.1.call-start
  7.2 1.9 %fusion.2 = f32[224]{0:T(256)S(1)} fusion(bf16[224,3584]{1,0:T(8,128)(2,1)} %param.8), kind=kLoop, calls=%fused_computation.5 | loop fusion | flops 2408224 | bytes 1606528 | tf_op jit(solution)/shard_map/reduce_sum | solution.py:18
  9.2 0.0 copy-done.2
  9.2 12.0 %all-gather = bf16[8,4,3584]{2,1,0:T(4,128)(2,1)} all-gather(bf16[1,4,3584]{2,1,0:T(4,128)(2,1)S(1)} %bitcast.12), channel_id=1, replica_groups=mesh['section'=4,'tensor'=8] {'tensor'}, dimensions={0}, use_global_device_ids=true | all-gather | bytes 258048 | tf_op jit(solution)/shard_map/all_gather | solution.py:10
  21.2 1.0 reshape.22
  22.2 0.0 copy-done
  22.2 0.0 copy-done.6
  22.2 1.2 fusion.5
  23.4 1.2 fusion.7
  24.5 0.0 all-reduce.4.cloned.1.call-update
  24.5 39.9 %psum.31 = f32[]{:T(128)} all-reduce(f32[]{:T(128)} %get-tuple-element.7), channel_id=1, replica_groups=mesh['section'=4,'tensor'=8] {'section','tensor'}, use_global_device_ids=true, to_apply=%region_9.0 | all-reduce | flops 1 | bytes 8 | tf_op jit(solution)/shard_map/psum | solution.py:19
  64.4 0.6 dynamic-slice
  65.7 14.0 %all-reduce.4.cloned.1.call-done = f32[32,3584]{1,0:T(8,128)} async-done(((f32[32,3584]{1,0:T(8,128)}), f32[32,3584]{1,0:T(8,128)}) %all-reduce.4.cloned.1.call-update) | async-done | bytes 458768
  79.7 0.9 constant_dynamic-slice_fusion
  80.6 19.6 %psum.28 = f32[4,3584]{1,0:T(4,128)S(1)} all-reduce(f32[4,3584]{1,0:T(4,128)S(1)} %constant_dynamic-slice_fusion), channel_id=1, replica_groups=mesh['section'=4,'tensor'=8] {'section'}, use_global_device_ids=true, to_apply=%region_1.0 | all-reduce | flops 14336 | bytes 114688 | tf_op jit(solution)/shard_map/psum | solution.py:28
  100.2 0.7 multiply_reduce_fusion
  101.0 9.6 %all-gather.1 = bf16[8,4,3584]{2,1,0:T(4,128)(2,1)} all-gather(bf16[1,4,3584]{2,1,0:T(4,128)(2,1)S(1)} %convert_bitcast_fusion), channel_id=1, replica_groups=mesh['section'=4,'tensor'=8] {'tensor'}, dimensions={0}, use_global_device_ids=true | all-gather | bytes 258048 | tf_op jit(solution)/shard_map/all_gather | solution.py:32
  110.6 1.0 reshape.24
  111.6 1.2 convolution_add_fusion.1
  112.8 1.8 %fusion = bf16[224,3584]{1,0:T(8,128)(2,1)} fusion(bf16[32,224]{1,0:T(8,128)(2,1)S(1)} %get-tuple-element.12, bf16[32,3584]{1,0:T(8,128)(2,1)S(1)} %reshape.24, bf16[224,3584]{1,0:T(8,128)(2,1)S(1)} %copy-done.1, f32[224]{0:T(256)S(1)} %add_sqrt_fusion, f32[224]{0:T(256)S(1)} %get-tuple-element.8), kind=kOutput, calls=%fused_computation.1 | convolution fusion | flops 55394304 | bytes 3456768 | tf_op jit(solution)/shard_map/dot_general | solution.py:35
  114.6 24.8 %all-reduce.1 = (f32[3584]{0:T(1024)}, f32[]{:T(128)}) all-reduce(f32[3584]{0:T(1024)S(1)} %copy-done.4, f32[]{:T(128)} %get-tuple-element.5), channel_id=1, replica_groups=mesh['section'=4,'tensor'=8] {'tensor'}, use_global_device_ids=true, to_apply=%region_5.0 | all-reduce | flops 3585 | bytes 28680 | tf_op jit(solution)/shard_map/psum | solution.py:31
  (12 shorter events, 0.0 us)
Async XLA Ops:
  7.2 15.0 %copy-start = (bf16[224,3584]{1,0:T(8,128)(2,1)S(1)}, bf16[224,3584]{1,0:T(8,128)(2,1)}, u32[]{:S(2)}) copy-start(bf16[224,3584]{1,0:T(8,128)(2,1)} %param.6) | copy-start | bytes 4816900
  7.2 2.0 %copy-start.2 = (bf16[4,3584]{1,0:T(4,128)(2,1)S(1)}, bf16[4,3584]{1,0:T(4,128)(2,1)}, u32[]{:S(2)}) copy-start(bf16[4,3584]{1,0:T(4,128)(2,1)} %param.5) | copy-start | bytes 86020
  7.2 15.0 %copy-start.6 = (f32[224]{0:T(256)S(1)}, f32[224]{0:T(256)}, u32[]{:S(2)}) copy-start(f32[224]{0:T(256)} %param.7) | copy-start | bytes 2692
  7.2 72.5 %all-reduce.4.cloned.1.call-start = ((), (), s32[]{:S(2)}) async-start(), calls=%async_computation | async-start | bytes 917504
  9.2 14.2 %copy-start.1 = (bf16[224,3584]{1,0:T(8,128)(2,1)S(1)}, bf16[224,3584]{1,0:T(8,128)(2,1)}, u32[]{:S(2)}) copy-start(bf16[224,3584]{1,0:T(8,128)(2,1)} %param.8) | copy-start | bytes 4816900
  23.4 41.1 %copy-start.7 = (u32[32]{0:T(128)S(1)}, u32[32]{0:T(128)}, u32[]{:S(2)}) copy-start(u32[32]{0:T(128)} %constant.13) | copy-start | bytes 388
  23.4 76.8 %copy-start.5 = (f32[3584]{0:T(1024)S(1)}, f32[3584]{0:T(1024)}, u32[]{:S(2)}) copy-start(f32[3584]{0:T(1024)} %param.9) | copy-start | bytes 43012
  100.9 13.6 %copy-start.3 = (f32[4,3584]{1,0:T(4,128)}, f32[4,3584]{1,0:T(4,128)S(1)}, u32[]{:S(2)}) copy-start(f32[4,3584]{1,0:T(4,128)S(1)} %get-tuple-element.11) | copy-start | bytes 172036
  112.8 1.8 %copy-start.4 = (f32[3584]{0:T(1024)S(1)}, f32[3584]{0:T(1024)}, u32[]{:S(2)}) copy-start(f32[3584]{0:T(1024)} %get-tuple-element.6) | copy-start | bytes 43012
Sparse Core Ops, SparseCore 0:
  24.7 54.9 all-reduce.3
where the time goes:
time: 149 us
  blocking collectives  106 us (71%)
  between operations  17.2 us (12%)
  waiting for transfers between devices  14 us (9%)
  matrix products  5.33 us (4%)
  local copies, waits for them, and re-layouts  3.52 us (2%)
  other arithmetic  2.7 us (2%)
    psum x1, blocking collectives, per_device(): penalty = lax.psum(jnp.sum(codes_f32 * dec_norm), ('section', 'tensor'))  39.9 us
    psum x1, blocking collectives, per_device(): lax.psum((jnp.sum(errors * errors), jnp.sum(errors, axis=0)), 'tensor')  24.8 us
    psum x1, blocking collectives, per_device(): shares = lax.psum(shares, 'section')  19.6 us
    unnamed x2, waiting for transfers between devices  14 us
    all_gather x1, blocking collectives, per_device(): stream = lax.all_gather(resid, 'tensor', axis=0, tiled=True)  12 us
    all_gather x1, blocking collectives, per_device(): lax.all_gather(errors.astype(jnp.bfloat16), 'tensor', axis=0, tiled=True)  9.61 us
    unnamed x20, local copies, waits for them, and re-layouts  3.52 us
  transfers between devices with their start and end apart: 1, of which 1 were waited for; matrix products, arithmetic and copies ran while one was open for 0% of the time, Pallas kernels for 0%

commit v1 on v0

--- a/solution.py
+++ b/solution.py
@@ -25,7 +25,8 @@
         scatter_dimension=0,
         tiled=True,
     )
-    shares = lax.psum(shares, "section")
+    shards = lax.all_gather(shares, "section", axis=0, tiled=False)
+    shares = shards.sum(axis=0)
     recon = shares + b_dec
     errors = recon - resid.astype(jnp.float32)
     squares, grad_b_dec = lax.psum((jnp.sum(errors * errors), jnp.sum(errors, axis=0)), "tensor")

time: 149 us -> 144 us (0.966)
  blocking collectives: 106 us -> 100 us
    psum x1 -> x0, blocking collectives: 19.6 us -> none  [per_device(): shares = lax.psum(shares, 'section')]
    all_gather x0 -> x1, blocking collectives: none -> 13.8 us  [per_device(): shards = lax.all_gather(shares, 'section', axis=0, tiled=False)]
    unnamed x20 -> x18, local copies, waits for them, and re-layouts: 3.52 us -> 3.52 us
where the time goes in v1:
time: 144 us
  blocking collectives  100 us (69%)
  between operations  17.2 us (12%)
  waiting for transfers between devices  14 us (10%)
  matrix products  5.33 us (4%)
  local copies, waits for them, and re-layouts  3.52 us (2%)
  other arithmetic  3.47 us (2%)
    psum x1, blocking collectives, per_device(): penalty = lax.psum(jnp.sum(codes_f32 * dec_norm), ('section', 'tensor'))  39.9 us
    psum x1, blocking collectives, per_device(): lax.psum((jnp.sum(errors * errors), jnp.sum(errors, axis=0)), 'tensor')  24.8 us
    unnamed x2, waiting for transfers between devices  14 us
    all_gather x1, blocking collectives, per_device(): shards = lax.all_gather(shares, 'section', axis=0, tiled=False)  13.8 us
    all_gather x1, blocking collectives, per_device(): stream = lax.all_gather(resid, 'tensor', axis=0, tiled=True)  12 us
    all_gather x1, blocking collectives, per_device(): lax.all_gather(errors.astype(jnp.bfloat16), 'tensor', axis=0, tiled=True)  9.52 us
    unnamed x18, local copies, waits for them, and re-layouts  3.52 us
  transfers between devices with their start and end apart: 1, of which 1 were waited for; matrix products, arithmetic and copies ran while one was open for 0% of the time, Pallas kernels for 0%

profile of v1, /device:TPU:0, one launch (start us, length us, event | category | flops | bytes accessed | tf_op | source)
XLA Modules:
  0.0 143.6 jit_solution(724535026031730684)
XLA Ops:
  7.2 0.0 copy-start
  7.2 0.0 copy-start.2
  7.2 0.0 copy-start.5
  7.2 0.0 all-reduce.4.cloned.1.call-start
  7.2 1.9 %fusion.2 = f32[224]{0:T(256)S(1)} fusion(bf16[224,3584]{1,0:T(8,128)(2,1)} %param.8), kind=kLoop, calls=%fused_computation.5 | loop fusion | flops 2408224 | bytes 1606528 | tf_op jit(solution)/shard_map/reduce_sum | solution.py:18
  9.2 0.0 copy-done.2
  9.2 12.0 %all-gather.1 = bf16[8,4,3584]{2,1,0:T(4,128)(2,1)} all-gather(bf16[1,4,3584]{2,1,0:T(4,128)(2,1)S(1)} %bitcast.14), channel_id=1, replica_groups=mesh['section'=4,'tensor'=8] {'tensor'}, dimensions={0}, use_global_device_ids=true | all-gather | bytes 258048 | tf_op jit(solution)/shard_map/all_gather | solution.py:10
  21.2 1.0 reshape.23
  22.2 0.0 copy-done
  22.2 0.0 copy-done.5
  22.2 1.2 fusion.5
  23.4 1.2 fusion.7
  24.5 0.0 all-reduce.4.cloned.1.call-update
  24.5 39.9 %psum.23 = f32[]{:T(128)} all-reduce(f32[]{:T(128)} %get-tuple-element.7), channel_id=1, replica_groups=mesh['section'=4,'tensor'=8] {'section','tensor'}, use_global_device_ids=true, to_apply=%region_9.0 | all-reduce | flops 1 | bytes 8 | tf_op jit(solution)/shard_map/psum | solution.py:19
  64.4 0.6 dynamic-slice
  65.7 14.0 %all-reduce.4.cloned.1.call-done = f32[32,3584]{1,0:T(8,128)} async-done(((f32[32,3584]{1,0:T(8,128)}), f32[32,3584]{1,0:T(8,128)}) %all-reduce.4.cloned.1.call-update) | async-done | bytes 458768
  79.7 0.9 dynamic-slice_bitcast_fusion
  80.6 13.8 %all-gather.2 = f32[4,4,3584]{2,1,0:T(4,128)S(1)} all-gather(f32[1,4,3584]{2,1,0:T(4,128)S(1)} %dynamic-slice_bitcast_fusion), channel_id=2, replica_groups=mesh['section'=4,'tensor'=8] {'section'}, dimensions={0}, use_global_device_ids=true | all-gather | bytes 286720 | tf_op jit(solution)/shard_map/all_gather | solution.py:28
  94.4 1.5 %multiply_reduce_fusion = (f32[]{:T(128)}, f32[3584]{0:T(1024)}, f32[4,3584]{1,0:T(4,128)S(1)}) fusion(bf16[4,3584]{1,0:T(4,128)(2,1)S(1)} %copy-done.2, f32[4,3584]{1,0:T(4,128)S(1)} %reduce_sum.54, f32[3584]{0:T(1024)} %param.9), kind=kLoop, calls=%fused_computation.11 | loop fusion | flops 82431 | bytes 172036 | tf_op jit(solution)/shard_map/reduce_sum | solution.py:32
  95.9 9.5 %all-gather.3 = bf16[8,4,3584]{2,1,0:T(4,128)(2,1)} all-gather(bf16[1,4,3584]{2,1,0:T(4,128)(2,1)S(1)} %convert_bitcast_fusion), channel_id=1, replica_groups=mesh['section'=4,'tensor'=8] {'tensor'}, dimensions={0}, use_global_device_ids=true | all-gather | bytes 258048 | tf_op jit(solution)/shard_map/all_gather | solution.py:33
  105.5 1.0 reshape.27
  106.5 1.2 convolution_add_fusion.1
  107.6 1.8 %fusion = bf16[224,3584]{1,0:T(8,128)(2,1)} fusion(bf16[32,224]{1,0:T(8,128)(2,1)S(1)} %get-tuple-element.12, bf16[32,3584]{1,0:T(8,128)(2,1)S(1)} %reshape.27, bf16[224,3584]{1,0:T(8,128)(2,1)S(1)} %copy-done.1, f32[224]{0:T(256)S(1)} %add_sqrt_fusion, f32[224]{0:T(256)S(1)} %get-tuple-element.8), kind=kOutput, calls=%fused_computation.1 | convolution fusion | flops 55394304 | bytes 3456768 | tf_op jit(solution)/shard_map/dot_general | solution.py:36
  109.4 24.8 %all-reduce.1 = (f32[3584]{0:T(1024)}, f32[]{:T(128)}) all-reduce(f32[3584]{0:T(1024)S(1)} %copy-done.4, f32[]{:T(128)} %get-tuple-element.5), channel_id=1, replica_groups=mesh['section'=4,'tensor'=8] {'tensor'}, use_global_device_ids=true, to_apply=%region_5.0 | all-reduce | flops 3585 | bytes 28680 | tf_op jit(solution)/shard_map/psum | solution.py:32
  (11 shorter events, 0.1 us)
Async XLA Ops:
  7.2 15.0 %copy-start = (bf16[224,3584]{1,0:T(8,128)(2,1)S(1)}, bf16[224,3584]{1,0:T(8,128)(2,1)}, u32[]{:S(2)}) copy-start(bf16[224,3584]{1,0:T(8,128)(2,1)} %param.6) | copy-start | bytes 4816900
  7.2 2.0 %copy-start.2 = (bf16[4,3584]{1,0:T(4,128)(2,1)S(1)}, bf16[4,3584]{1,0:T(4,128)(2,1)}, u32[]{:S(2)}) copy-start(bf16[4,3584]{1,0:T(4,128)(2,1)} %param.5) | copy-start | bytes 86020
  7.2 15.0 %copy-start.5 = (f32[224]{0:T(256)S(1)}, f32[224]{0:T(256)}, u32[]{:S(2)}) copy-start(f32[224]{0:T(256)} %param.7) | copy-start | bytes 2692
  7.2 72.5 %all-reduce.4.cloned.1.call-start = ((), (), s32[]{:S(2)}) async-start(), calls=%async_computation | async-start | bytes 917504
  9.2 14.2 %copy-start.1 = (bf16[224,3584]{1,0:T(8,128)(2,1)S(1)}, bf16[224,3584]{1,0:T(8,128)(2,1)}, u32[]{:S(2)}) copy-start(bf16[224,3584]{1,0:T(8,128)(2,1)} %param.8) | copy-start | bytes 4816900
  23.4 41.1 %copy-start.6 = (u32[32]{0:T(128)S(1)}, u32[32]{0:T(128)}, u32[]{:S(2)}) copy-start(u32[32]{0:T(128)} %constant.13) | copy-start | bytes 388
  95.9 13.5 %copy-start.3 = (f32[4,3584]{1,0:T(4,128)}, f32[4,3584]{1,0:T(4,128)S(1)}, u32[]{:S(2)}) copy-start(f32[4,3584]{1,0:T(4,128)S(1)} %get-tuple-element.11) | copy-start | bytes 172036
  107.6 1.8 %copy-start.4 = (f32[3584]{0:T(1024)S(1)}, f32[3584]{0:T(1024)}, u32[]{:S(2)}) copy-start(f32[3584]{0:T(1024)} %get-tuple-element.6) | copy-start | bytes 43012
Sparse Core Ops, SparseCore 0:
  24.7 54.9 all-reduce.3
